TPU v7x, 256 devices: a whole 4x4x8 slice. The times are simulated.
256 devices in a mesh: cal: 64 (over z, y, core), gr: 4 (over x).
Axes of the slice: x: 4, y: 4, z: 8, core: 2. Of those that a mesh axis runs over, the one named last changes fastest.
Arguments:
- features: bfloat16 [131072, 4096], P('cal', 'gr'), may hold values from -6 to 6
- coef: bfloat16 [4096], P('gr'), may hold values from -0.09375 to 0.09375
- log_exposure: float32 [131072], P('cal'), may hold values from -0.7 to 0.7
- claims: float32 [131072], P('cal'), may hold values from 0 to 4
- cluster_id: int32 [131072], P('cal'), may hold values from 0 to 1023
- period: int32 [131072], P('cal'), may hold values from 0 to 127, as said below
- period_effect: float32 [128], replicated, may hold values from -0.5 to 0.5
Outputs:
- meat: float32 [4096, 4096], P('cal', 'gr')
Inputs may be any that keep to these rules, and one draw needn't show every extreme that they name: `period`: rows of index d of cal lie in periods d * 2 to (d + 1) * 2 - 1.
All inputs are finite; a program needn't handle non-finite values.
Results may differ from a plain program's by a relative error of at most 0.0044.
Values sent between devices are 32-bit elements; how exact they have to be, the bound alone decides.
A program may use at most 64 MiB of HBM per device.

v0:
```python
import jax
import jax.numpy as jnp
from jax import lax
from jax.sharding import PartitionSpec as P

CL_DEV = 16


def per_device(features, coef, log_exposure, claims, cluster_id, period, period_effect):
    rows_here = features.shape[0]
    width = features.shape[1]
    n_cal = lax.axis_size("cal")
    clusters = CL_DEV * n_cal
    local_lin = jnp.dot(features, coef, preferred_element_type=jnp.float32)
    linear = lax.psum(local_lin, "gr")
    periods = period_effect.shape[0]
    table = jnp.where(
        period[:, None] == jnp.arange(periods, dtype=jnp.int32)[None, :],
        period_effect[None, :],
        jnp.float32(0.0),
    )
    shift = jnp.sum(table, axis=1)
    resid = (claims - jnp.exp(linear + log_exposure + shift)).astype(jnp.bfloat16)
    block = min(512, rows_here)
    count = rows_here // block
    feats = features.reshape(count, block, width)
    res_b = resid.reshape(count, block)
    ids_b = cluster_id.reshape(count, block)
    cluster_range = jnp.arange(clusters, dtype=jnp.int32)

    def step(carry, item):
        feat_blk, res_blk, id_blk = item
        picks = jnp.where(
            id_blk[:, None] == cluster_range[None, :], res_blk[:, None], jnp.bfloat16(0.0)
        )
        term = lax.dot_general(
            picks, feat_blk, (((0,), (0,)), ((), ())), preferred_element_type=jnp.float32
        )
        return (carry + term, None)

    partial_scores, _ = lax.scan(
        step, jnp.zeros((clusters, width), jnp.float32), (feats, res_b, ids_b)
    )
    owned = lax.psum_scatter(partial_scores, "cal", scatter_dimension=0, tiled=True)
    full_scores = lax.all_gather(owned, "gr", axis=1, tiled=True)
    scale = jnp.float32(1.0) / jnp.float32(rows_here * n_cal)
    meat_block = lax.psum_scatter(
        lax.dot_general(
            full_scores,
            owned,
            (((0,), (0,)), ((), ())),
            precision=lax.Precision.HIGHEST,
            preferred_element_type=jnp.float32,
        ),
        "cal",
        scatter_dimension=0,
        tiled=True,
    )
    return meat_block * scale


def solution(mesh):
    placed = (P("cal", "gr"), P("gr"), P("cal"), P("cal"), P("cal"), P("cal"), P())
    return jax.shard_map(
        per_device, mesh=mesh, in_specs=placed, out_specs=P("cal", "gr"), check_vma=False
    )
```

profile of v0, /device:TPU:2, one launch (start us, length us, event | category | flops | bytes accessed | tf_op | source)
XLA Modules:
  0.0 415.5 jit_solution(18031180852784625165)
XLA Ops:
  6.5 0.0 copy-start
  6.5 0.0 reduce-scatter.3.cloned.1.call-start
  6.6 0.7 reshape.19
  7.3 3.4 fusion.11
  10.7 10.1 %psum.7 = f32[2048]{0:T(1024)S(1)} all-reduce(f32[2048]{0:T(1024)S(1)} %bitcast.16), channel_id=1, replica_groups=mesh['cal'=64,'gr'=4] {'gr'}, use_global_device_ids=true, to_apply=%region_0.0 | all-reduce | flops 2048 | bytes 16384 | tf_op jit(solution)/shard_map/psum | solution.py:15
  20.7 0.0 copy-done
  20.8 0.0 copy-done.4
  20.8 0.0 copy-done.1
  20.8 0.6 select_reduce_fusion
  21.4 0.0 copy-done.2
  21.4 0.0 copy-done.3
  21.5 22.3 %while.11 = (s32[]{:T(128)}, f32[1024,1024]{1,0:T(8,128)}, s32[4,512]{1,0:T(4,128)S(1)}, bf16[4,512]{1,0:T(4,128)(2,1)S(1)}, bf16[4,512,1024]{2,1,0:T(8,128)(2,1)}, /*index=5*/s32[]{:T(128)}, s32[]{:T(128)}) while((s32[]{:T(128)}, f32[1024,1024]{1,0:T(8,128)}, s32[4,512]{1,0:T(4,128)S(1)}, bf16[4,512]{1,0:T(4,128)(2,1)S(1)}, ...), condition=%wide.region_3.4_spmd.clone, body=%wide.region_2.3_spmd.clone.sunk | while | flops 1076887552 | bytes 9446507 | solution.py:41
  21.5 4.6 %select_add_fusion.2 = f32[1024,1024]{1,0:T(8,128)} fusion(f32[1024,1024]{1,0:T(8,128)} %get-tuple-element.107, pred[]{:T(512)S(6)} %compare.3, bf16[4,512,1024]{2,1,0:T(8,128)(2,1)} %get-tuple-element.117, s32[]{:T(128)S(6)} %copy.10, s32[512]{0:T(512)S(1)} %bitcast.15, bf16[512]{0:T(512)(128)(2,1)S(1)} %dynamic-slice_reduce_fusion.2), kind=kOutput, calls=%fused_computation.1.clone.1 | convolution fusion | flops 1076887552 | bytes 9440261 | tf_op jit(solution)/shard_map/while/body/eval_jaxpr/dot_general | solution.py:36
  26.1 5.9 %select_add_fusion.2 = f32[1024,1024]{1,0:T(8,128)} fusion(f32[1024,1024]{1,0:T(8,128)} %get-tuple-element.107, pred[]{:T(512)S(6)} %compare.3, bf16[4,512,1024]{2,1,0:T(8,128)(2,1)} %get-tuple-element.117, s32[]{:T(128)S(6)} %copy.10, s32[512]{0:T(512)S(1)} %bitcast.15, bf16[512]{0:T(512)(128)(2,1)S(1)} %dynamic-slice_reduce_fusion.2), kind=kOutput, calls=%fused_computation.1.clone.1 | convolution fusion | flops 1076887552 | bytes 9440261 | tf_op jit(solution)/shard_map/while/body/eval_jaxpr/dot_general | solution.py:36
  32.0 5.9 %select_add_fusion.2 = f32[1024,1024]{1,0:T(8,128)} fusion(f32[1024,1024]{1,0:T(8,128)} %get-tuple-element.107, pred[]{:T(512)S(6)} %compare.3, bf16[4,512,1024]{2,1,0:T(8,128)(2,1)} %get-tuple-element.117, s32[]{:T(128)S(6)} %copy.10, s32[512]{0:T(512)S(1)} %bitcast.15, bf16[512]{0:T(512)(128)(2,1)S(1)} %dynamic-slice_reduce_fusion.2), kind=kOutput, calls=%fused_computation.1.clone.1 | convolution fusion | flops 1076887552 | bytes 9440261 | tf_op jit(solution)/shard_map/while/body/eval_jaxpr/dot_general | solution.py:36
  37.9 5.9 %select_add_fusion.2 = f32[1024,1024]{1,0:T(8,128)} fusion(f32[1024,1024]{1,0:T(8,128)} %get-tuple-element.107, pred[]{:T(512)S(6)} %compare.3, bf16[4,512,1024]{2,1,0:T(8,128)(2,1)} %get-tuple-element.117, s32[]{:T(128)S(6)} %copy.10, s32[512]{0:T(512)S(1)} %bitcast.15, bf16[512]{0:T(512)(128)(2,1)S(1)} %dynamic-slice_reduce_fusion.2), kind=kOutput, calls=%fused_computation.1.clone.1 | convolution fusion | flops 1076887552 | bytes 9440261 | tf_op jit(solution)/shard_map/while/body/eval_jaxpr/dot_general | solution.py:36
  43.8 0.0 reduce-scatter.3.cloned.1.call-update
  43.8 0.0 reduce-scatter.5.cloned.1.call-start
  43.9 145.9 %reduce-scatter.3.cloned.1.call-done = f32[16,1024]{1,0:T(8,128)} async-done(((f32[1024,1024]{1,0:T(8,128)}), f32[16,1024]{1,0:T(8,128)}) %reduce-scatter.3.cloned.1.call-update) | async-done | bytes 65552 | tf_op jit(solution)/shard_map/reduce_scatter | solution.py:44
  189.7 12.6 %all_gather.3 = f32[16,4096]{1,0:T(8,128)S(1)} all-gather(f32[16,1024]{1,0:T(8,128)} %reduce-scatter.3.cloned.1.call-done), channel_id=1, replica_groups=mesh['cal'=64,'gr'=4] {'gr'}, dimensions={1}, use_global_device_ids=true | all-gather | bytes 327680 | tf_op jit(solution)/shard_map/all_gather | solution.py:45
  202.3 16.7 %fusion.12 = f32[4096,1024]{1,0:T(8,128)} fusion(f32[16,4096]{1,0:T(8,128)S(1)} %all_gather.3, f32[16,1024]{1,0:T(8,128)} %reduce-scatter.3.cloned.1.call-done), kind=kOutput, calls=%fused_computation.18 | convolution fusion | flops 805306368 | bytes 17104896 | tf_op jit(solution)/shard_map/dot_general | solution.py:48
  219.0 0.0 reduce-scatter.5.cloned.1.call-update
  219.0 187.9 %reduce-scatter.5.cloned.1.call-done = f32[64,1024]{1,0:T(8,128)} async-done(((f32[4096,1024]{1,0:T(8,128)}), f32[64,1024]{1,0:T(8,128)}) %reduce-scatter.5.cloned.1.call-update) | async-done | bytes 262160 | tf_op jit(solution)/shard_map/reduce_scatter | solution.py:47
  407.0 1.7 broadcast_multiply_fusion
  (16 shorter events, 0.2 us)
Async XLA Ops:
  6.5 14.2 %copy-start = (s32[2048]{0:T(1024)S(1)}, s32[2048]{0:T(1024)}, u32[]{:S(2)}) copy-start(s32[2048]{0:T(1024)} %param.13) | copy-start | bytes 24580
  6.5 14.2 %copy-start.4 = (f32[128]{0:T(128)S(1)}, f32[128]{0:T(128)}, u32[]{:S(2)}) copy-start(f32[128]{0:T(128)} %param.15) | copy-start | bytes 1540
  6.5 14.2 %copy-start.1 = (s32[2048]{0:T(1024)S(1)}, s32[2048]{0:T(1024)}, u32[]{:S(2)}) copy-start(s32[2048]{0:T(1024)} %param.14) | copy-start | bytes 24580
  6.5 14.9 %copy-start.2 = (f32[2048]{0:T(1024)S(1)}, f32[2048]{0:T(1024)}, u32[]{:S(2)}) copy-start(f32[2048]{0:T(1024)} %param.12) | copy-start | bytes 24580
  6.5 14.9 %copy-start.3 = (f32[2048]{0:T(1024)S(1)}, f32[2048]{0:T(1024)}, u32[]{:S(2)}) copy-start(f32[2048]{0:T(1024)} %param.11) | copy-start | bytes 24580
  6.5 183.2 %reduce-scatter.3.cloned.1.call-start = ((), (), s32[]{:S(2)}) async-start(), calls=%async_computation.2 | async-start | bytes 4259840 | tf_op jit(solution)/shard_map/reduce_scatter | solution.py:44
  43.8 363.2 %reduce-scatter.5.cloned.1.call-start = ((), (), s32[]{:S(2)}) async-start(), calls=%async_computation.3 | async-start | bytes 17039360 | tf_op jit(solution)/shard_map/reduce_scatter | solution.py:47
Sparse Core Ops, SparseCore 0:
  43.9 145.7 reduce-scatter.2
  219.1 187.7 reduce-scatter.4
where the time goes:
time: 416 us; the launch traced here: 415 us
  waiting for transfers between devices  334 us (80%)
  matrix products  42.2 us (10%)
  blocking collectives  22.6 us (5%)
  between operations  13.5 us (3%)
    reduce_scatter x1, waiting for transfers between devices, per_device(): lax.psum_scatter(lax.dot_general(full_scores, owned, (((0,), (0,)), ((),...  188 us
    reduce_scatter x1, waiting for transfers between devices, per_device(): lax.psum_scatter(partial_scores, 'cal', scatter_dimension=0, tiled=True)  146 us
    dot_general x4, matrix products, step(): lax.dot_general(picks, feat_blk, (((0,), (0,)), ((), ())), preferred_elem...  22.2 us
    dot_general x1, matrix products, per_device(): lax.dot_general(full_scores, owned, (((0,), (0,)), ((), ())), precision=l...  16.7 us
    all_gather x1, blocking collectives, per_device(): full_scores = lax.all_gather(owned, 'gr', axis=1, tiled=True)  12.6 us
    psum x1, blocking collectives, per_device(): linear = lax.psum(local_lin, 'gr')  10.1 us
  transfers between devices with their start and end apart: 2, of which 2 were waited for; matrix products, arithmetic and copies ran while one was open for 0% of the time, Pallas kernels for 0%

commit v1 on v0

--- a/solution.py
+++ b/solution.py
@@ -42,7 +42,16 @@
         step, jnp.zeros((clusters, width), jnp.float32), (feats, res_b, ids_b)
     )
     owned = lax.psum_scatter(partial_scores, "cal", scatter_dimension=0, tiled=True)
-    full_scores = lax.all_gather(owned, "gr", axis=1, tiled=True)
+    ways = lax.axis_size("gr")
+    up = [(d, (d + 1) % ways) for d in range(ways)]
+    down = [(d, (d - 1) % ways) for d in range(ways)]
+    earlier, later = ([owned], [owned])
+    for __2 in range(ways // 2):
+        earlier.append(lax.ppermute(earlier[-1], "gr", up))
+    for __2 in range((ways - 1) // 2):
+        later.append(lax.ppermute(later[-1], "gr", down))
+    line = jnp.concatenate([*earlier[::-1], *later[1:]], axis=1)
+    full_scores = jnp.roll(line, (lax.axis_index("gr") - ways // 2) * owned.shape[1], axis=1)
     scale = jnp.float32(1.0) / jnp.float32(rows_here * n_cal)
     meat_block = lax.psum_scatter(
         lax.dot_general(

time: 416 us -> 416 us (level)
  blocking collectives: 22.6 us -> 10.1 us
  waiting for transfers between devices: 334 us -> 341 us
    all_gather x1 -> x0, blocking collectives: 12.6 us -> none  [per_device(): full_scores = lax.all_gather(owned, 'gr', axis=1, tiled=True)]
    ppermute x0 -> x3, waiting for transfers between devices: none -> 6.06 us  [the longest x2 5.25 us: per_device(): earlier.append(lax.ppermute(earlier[-1], 'gr', up))]
  transfers between devices with their start and end apart: 2 -> 5, of which waited for: 2 -> 5; matrix products, arithmetic and copies ran while one was open for 0% -> 0% of each run, Pallas kernels for 0% -> 0%
where the time goes in v1:
time: 416 us
  waiting for transfers between devices  341 us (82%)
  matrix products  42.3 us (10%)
  between operations  13.5 us (3%)
  blocking collectives  10.1 us (2%)
    reduce_scatter x1, waiting for transfers between devices, per_device(): lax.psum_scatter(lax.dot_general(full_scores, owned, (((0,), (0,)), ((),...  189 us
    reduce_scatter x1, waiting for transfers between devices, per_device(): lax.psum_scatter(partial_scores, 'cal', scatter_dimension=0, tiled=True)  146 us
    dot_general x4, matrix products, step(): lax.dot_general(picks, feat_blk, (((0,), (0,)), ((), ())), preferred_elem...  22.2 us
    dot_general x1, matrix products, per_device(): lax.dot_general(full_scores, owned, (((0,), (0,)), ((), ())), precision=l...  16.7 us
    psum x1, blocking collectives, per_device(): linear = lax.psum(local_lin, 'gr')  10.1 us
  transfers between devices with their start and end apart: 5, of which 5 were waited for; matrix products, arithmetic and copies ran while one was open for 0% of the time, Pallas kernels for 0%

profile of v1, /device:TPU:2, one launch (start us, length us, event | category | flops | bytes accessed | tf_op | source)
XLA Modules:
  0.0 415.7 jit_solution(13559465136922048671)
XLA Ops:
  6.5 0.0 reduce-scatter.3.cloned.1.call-start
  6.6 0.7 reshape.19
  7.3 3.4 fusion.14
  10.7 10.1 %psum.7 = f32[2048]{0:T(1024)S(1)} all-reduce(f32[2048]{0:T(1024)S(1)} %bitcast.15), channel_id=1, replica_groups=mesh['cal'=64,'gr'=4] {'gr'}, use_global_device_ids=true, to_apply=%region_0.0 | all-reduce | flops 2048 | bytes 16384 | tf_op jit(solution)/shard_map/psum | solution.py:15
  20.8 0.6 select_reduce_fusion
  21.5 22.4 %while.11 = (s32[]{:T(128)}, f32[1024,1024]{1,0:T(8,128)}, s32[4,512]{1,0:T(4,128)S(1)}, bf16[4,512]{1,0:T(4,128)(2,1)S(1)}, bf16[4,512,1024]{2,1,0:T(8,128)(2,1)}, /*index=5*/s32[]{:T(128)}, s32[]{:T(128)}) while((s32[]{:T(128)}, f32[1024,1024]{1,0:T(8,128)}, s32[4,512]{1,0:T(4,128)S(1)}, bf16[4,512]{1,0:T(4,128)(2,1)S(1)}, ...), condition=%wide.region_3.4_spmd.clone, body=%wide.region_2.3_spmd.clone.sunk | while | flops 1076887552 | bytes 9446507 | solution.py:41
  21.5 4.6 %select_add_fusion.2 = f32[1024,1024]{1,0:T(8,128)} fusion(f32[1024,1024]{1,0:T(8,128)} %get-tuple-element.107, pred[]{:T(512)S(6)} %compare.4, bf16[4,512,1024]{2,1,0:T(8,128)(2,1)} %get-tuple-element.117, s32[]{:T(128)S(6)} %copy.10, s32[512]{0:T(512)S(1)} %bitcast.14, bf16[512]{0:T(512)(128)(2,1)S(1)} %dynamic-slice_reduce_fusion.2), kind=kOutput, calls=%fused_computation.1.clone.1 | convolution fusion | flops 1076887552 | bytes 9440261 | tf_op jit(solution)/shard_map/while/body/eval_jaxpr/dot_general | solution.py:36
  26.1 5.9 %select_add_fusion.2 = f32[1024,1024]{1,0:T(8,128)} fusion(f32[1024,1024]{1,0:T(8,128)} %get-tuple-element.107, pred[]{:T(512)S(6)} %compare.4, bf16[4,512,1024]{2,1,0:T(8,128)(2,1)} %get-tuple-element.117, s32[]{:T(128)S(6)} %copy.10, s32[512]{0:T(512)S(1)} %bitcast.14, bf16[512]{0:T(512)(128)(2,1)S(1)} %dynamic-slice_reduce_fusion.2), kind=kOutput, calls=%fused_computation.1.clone.1 | convolution fusion | flops 1076887552 | bytes 9440261 | tf_op jit(solution)/shard_map/while/body/eval_jaxpr/dot_general | solution.py:36
  32.0 5.9 %select_add_fusion.2 = f32[1024,1024]{1,0:T(8,128)} fusion(f32[1024,1024]{1,0:T(8,128)} %get-tuple-element.107, pred[]{:T(512)S(6)} %compare.4, bf16[4,512,1024]{2,1,0:T(8,128)(2,1)} %get-tuple-element.117, s32[]{:T(128)S(6)} %copy.10, s32[512]{0:T(512)S(1)} %bitcast.14, bf16[512]{0:T(512)(128)(2,1)S(1)} %dynamic-slice_reduce_fusion.2), kind=kOutput, calls=%fused_computation.1.clone.1 | convolution fusion | flops 1076887552 | bytes 9440261 | tf_op jit(solution)/shard_map/while/body/eval_jaxpr/dot_general | solution.py:36
  38.0 5.9 %select_add_fusion.2 = f32[1024,1024]{1,0:T(8,128)} fusion(f32[1024,1024]{1,0:T(8,128)} %get-tuple-element.107, pred[]{:T(512)S(6)} %compare.4, bf16[4,512,1024]{2,1,0:T(8,128)(2,1)} %get-tuple-element.117, s32[]{:T(128)S(6)} %copy.10, s32[512]{0:T(512)S(1)} %bitcast.14, bf16[512]{0:T(512)(128)(2,1)S(1)} %dynamic-slice_reduce_fusion.2), kind=kOutput, calls=%fused_computation.1.clone.1 | convolution fusion | flops 1076887552 | bytes 9440261 | tf_op jit(solution)/shard_map/while/body/eval_jaxpr/dot_general | solution.py:36
  43.8 0.0 reduce-scatter.3.cloned.1.call-update
  43.9 0.0 reduce-scatter.5.cloned.1.call-start
  43.9 145.9 %reduce-scatter.3.cloned.1.call-done = f32[16,1024]{1,0:T(8,128)} async-done(((f32[1024,1024]{1,0:T(8,128)}), f32[16,1024]{1,0:T(8,128)}) %reduce-scatter.3.cloned.1.call-update) | async-done | bytes 65552 | tf_op jit(solution)/shard_map/reduce_scatter | solution.py:44
  189.8 1.5 collective-permute-start
  191.3 3.0 collective-permute-done
  194.3 1.5 collective-permute-start.1
  195.8 0.6 collective-permute-start.2
  196.3 2.2 collective-permute-done.1
  198.6 0.8 constant_dynamic-update-slice_fusion.5
  199.5 0.8 collective-permute-done.2
  200.3 0.8 constant_dynamic-update-slice_fusion.1
  201.1 16.7 %fusion.11 = f32[4096,1024]{1,0:T(8,128)} fusion(f32[16,1024]{1,0:T(8,128)} %reduce-scatter.3.cloned.1.call-done, f32[16,8192]{1,0:T(8,128)S(1)} %constant_dynamic-update-slice_fusion, s32[]{:T(128)S(6)} %select_n.23), kind=kOutput, calls=%fused_computation.15 | convolution fusion | flops 805306368 | bytes 17104900 | tf_op jit(solution)/shard_map/dot_general | solution.py:57
  217.8 189.4 %reduce-scatter.5.cloned.1.call-done = f32[64,1024]{1,0:T(8,128)} async-done(((f32[4096,1024]{1,0:T(8,128)}), f32[64,1024]{1,0:T(8,128)}) %reduce-scatter.5.cloned.1.call-update) | async-done | bytes 262160 | tf_op jit(solution)/shard_map/reduce_scatter | solution.py:56
  407.2 1.7 broadcast_multiply_fusion
  (29 shorter events, 0.2 us)
Async XLA Ops:
  6.5 14.2 %copy-start = (s32[2048]{0:T(1024)S(1)}, s32[2048]{0:T(1024)}, u32[]{:S(2)}) copy-start(s32[2048]{0:T(1024)} %param.13) | copy-start | bytes 24580
  6.5 14.2 %copy-start.4 = (f32[128]{0:T(128)S(1)}, f32[128]{0:T(128)}, u32[]{:S(2)}) copy-start(f32[128]{0:T(128)} %param.15) | copy-start | bytes 1540
  6.5 14.2 %copy-start.1 = (s32[2048]{0:T(1024)S(1)}, s32[2048]{0:T(1024)}, u32[]{:S(2)}) copy-start(s32[2048]{0:T(1024)} %param.14) | copy-start | bytes 24580
  6.5 14.9 %copy-start.2 = (f32[2048]{0:T(1024)S(1)}, f32[2048]{0:T(1024)}, u32[]{:S(2)}) copy-start(f32[2048]{0:T(1024)} %param.12) | copy-start | bytes 24580
  6.5 14.9 %copy-start.3 = (f32[2048]{0:T(1024)S(1)}, f32[2048]{0:T(1024)}, u32[]{:S(2)}) copy-start(f32[2048]{0:T(1024)} %param.11) | copy-start | bytes 24580
  6.5 183.3 %reduce-scatter.3.cloned.1.call-start = ((), (), s32[]{:S(2)}) async-start(), calls=%async_computation.2 | async-start | bytes 4259840 | tf_op jit(solution)/shard_map/reduce_scatter | solution.py:44
  43.9 363.4 %reduce-scatter.5.cloned.1.call-start = ((), (), s32[]{:S(2)}) async-start(), calls=%async_computation.3 | async-start | bytes 17039360 | tf_op jit(solution)/shard_map/reduce_scatter | solution.py:56
  189.8 4.5 %collective-permute-start = (f32[16,1024]{1,0:T(8,128)}, f32[16,1024]{1,0:T(8,128)S(1)}, u32[]{:S(2)}, u32[]{:S(2)}) collective-permute-start(f32[16,1024]{1,0:T(8,128)} %reduce-scatter.3.cloned.1.call-done), channel_id=1, source_target_pairs={{0,1},{1,2},{2,3},{3,0},{4,5},{5,6},{6,7},{7,4},{8,9},{9,10},{10,1... | collective-permute-start | bytes 196616 | tf_op jit(solution)/shard_map/ppermute | solution.py:50
  194.3 4.3 %collective-permute-start.1 = (f32[16,1024]{1,0:T(8,128)S(1)}, f32[16,1024]{1,0:T(8,128)S(1)}, u32[]{:S(2)}, u32[]{:S(2)}) collective-permute-start(f32[16,1024]{1,0:T(8,128)S(1)} %collective-permute-done), channel_id=1, source_target_pairs={{0,1},{1,2},{2,3},{3,0},{4,5},{5,6},{6,7},{7,4},{8,9},{9,10},{10,1... | collective-permute-start | bytes 196616 | tf_op jit(solution)/shard_map/ppermute | solution.py:50
  195.8 4.5 %collective-permute-start.2 = (f32[16,1024]{1,0:T(8,128)}, f32[16,1024]{1,0:T(8,128)S(1)}, u32[]{:S(2)}, u32[]{:S(2)}) collective-permute-start(f32[16,1024]{1,0:T(8,128)} %reduce-scatter.3.cloned.1.call-done), channel_id=1, source_target_pairs={{0,3},{1,0},{2,1},{3,2},{4,7},{5,4},{6,5},{7,6},{8,11},{9,8},{10,9... | collective-permute-start | bytes 196616 | tf_op jit(solution)/shard_map/ppermute | solution.py:52
Sparse Core Ops, SparseCore 0:
  44.0 145.8 reduce-scatter.2
  218.0 189.2 reduce-scatter.4
